TPU v7x, 512 devices: a whole 4x4x16 slice. The times are simulated.
512 devices in a mesh: site: 32 (over x_hi, z), expert: 16 (over y, x_lo, core).
Axes of the slice: x: 4 (x_hi: 2, x_lo: 2; x = x_hi * 2 + x_lo), y: 4, z: 16, core: 2. Of those that a mesh axis runs over, the one named last changes fastest.
Arguments:
- out_grads: bfloat16 [2, 32, 2048, 1024], P(None, 'site', 'expert'), may hold values from -6 to 6
- routes: int32 [2, 32, 2048, 1], P(None, 'site', 'expert'), may hold values from 0 to 15; in each aligned block of 128 rows (0 to 127, 128 to 255, ..., all dimensions but the last counted through in order) at most 16 rows name the same one
- hiddens: bfloat16 [2, 32, 16, 256, 512], P(None, 'site', 'expert'), may hold values from -6 to 6
- weights: bfloat16 [32, 16, 512, 1024], P('site', 'expert'), may hold values from -6 to 6
- tracker_offset: bfloat16 [32, 16, 512, 1024], P('site', 'expert'), may hold values from -20 to 20
- partner_bits: int32 [32, 2], P('site'), may hold values from 0 to 1, as said below
Outputs:
- new_weights: bfloat16 [32, 16, 512, 1024], P('site', 'expert')
Inputs may be any that keep to these rules, and one draw needn't show every extreme that they name: `routes`: among the 128 tokens of one device in a step no expert is named more than 16 times, a bound that some block reaches. `partner_bits`: site 0 and site 32 - 1 each take the partner ahead in exactly one of the two rounds.
All inputs are finite; a program needn't handle non-finite values.
Results may differ from a plain program's by a relative error of at most 0.0095.
Values may be sent and summed in bfloat16 or wider, within the bound.
A program may use at most 64 MiB of HBM per device.

v0:
```python
import functools
import math

import jax
import jax.numpy as jnp
from jax import lax
from jax.experimental import pallas as pl
from jax.experimental.pallas import tpu as pltpu
from jax.sharding import PartitionSpec as P

MESH = pl.DeviceIdType.MESH
F32 = jnp.float32
BF16 = jnp.bfloat16

coef_a = 3.4445
coef_b = -4.775
coef_c = 2.0315
step_scale = 32.0
HOPS = (1, 2, 4)
BASE = (0, 1, 3)
RELAY = (0, 0, 1)
CHUNK = 256


def dot_nn(a, b):
    return lax.dot_general(a, b, (((1,), (0,)), ((), ())), preferred_element_type=F32)


def dot_nt(a, b):
    return lax.dot_general(a, b, (((1,), (1,)), ((), ())), preferred_element_type=F32)


def dot_tn(a, b):
    return lax.dot_general(a, b, (((0,), (0,)), ((), ())), preferred_element_type=F32)


def kernel(
    n_sites, n_experts, chunk,
    og_hbm, routes_ref, hid_hbm, w_hbm, off_hbm, bits_ref, out_ref,
    og, hid, wt, off, placed, arrived, grad, sent, relay, near, tnorm, xmid, moved,
    gram, gram_b, poly, fro,
    load_sem, a2a_send, a2a_recv, hop_send, hop_recv, turn,
):
    site = lax.axis_index("site")
    me = lax.axis_index("expert")
    ff, features = w_hbm.shape
    chunks = features // chunk
    rows = hid.shape[1]
    slots = rows // n_experts
    tokens = og.shape[1]

    def cols(c):
        return pl.ds(pl.multiple_of(c * chunk, chunk), chunk)

    ring = n_sites // 2
    lane = site // ring
    spot = lax.rem(site, ring)

    far = HOPS[-1]
    core = lax.rem(me, 2)
    chip = me // 2
    n_chips = n_experts // 2

    def ring_at(distance, cross=0):
        return lax.rem(lane + cross, 2) * ring + lax.rem(spot + (distance + ring), ring)

    loads = [pltpu.make_async_copy(og_hbm.at[k], og.at[k], load_sem.at[k]) for k in range(2)]
    loads += [pltpu.make_async_copy(hid_hbm.at[k], hid.at[k], load_sem.at[2 + k]) for k in range(2)]

    def off_load(c):
        return pltpu.make_async_copy(off_hbm.at[:, cols(c)], off.at[c], load_sem.at[4 + c])

    def w_load(c):
        return pltpu.make_async_copy(w_hbm.at[:, cols(c)], wt.at[c], load_sem.at[4 + chunks + c])

    loads[0].start()
    loads[2].start()
    for c in range(chunks):
        off_load(c).start()
    loads[1].start()
    loads[3].start()
    for c in range(chunks):
        w_load(c).start()

    barrier = pltpu.get_barrier_semaphore()
    def greet(device_id):
        pl.semaphore_signal(barrier, inc=1, device_id=device_id, device_id_type=MESH)

    for way in (1, -1):
        greet({"site": ring_at(way)})
    pl.when(spot < far)(lambda: greet({"site": ring_at(-1, 1)}))
    pl.when(spot >= ring - far)(lambda: greet({"site": ring_at(1, 1)}))

    @pl.loop(1, n_experts)
    def _(d):
        greet({"expert": lax.rem(me + d, n_experts)})

    crossings = jnp.where(lax.rem(spot + 1, ring) < far, 1, 0) + jnp.where(lax.rem(ring - spot, ring) < far, 1, 0)

    def place(k):
        routing = routes_ref[pl.ds(k, 1), :]
        experts = lax.broadcasted_iota(jnp.int32, (n_experts, tokens), 0)
        owned = jnp.where(experts == routing, 1.0, 0.0)
        early = lax.broadcasted_iota(jnp.int32, (tokens, tokens), 0)
        late = lax.broadcasted_iota(jnp.int32, (tokens, tokens), 1)
        before = jnp.where(early < late, 1.0, 0.0).astype(BF16)
        earlier = dot_nn(owned.astype(BF16), before)
        position = jnp.sum(earlier * owned, axis=0, keepdims=True)
        target = routing.astype(F32) * float(slots) + position
        place_of = lax.broadcasted_iota(jnp.int32, (rows, tokens), 0).astype(F32)
        selector = jnp.where(place_of == target, 1.0, 0.0).astype(BF16)
        placed[k] = dot_nn(selector, og[k]).astype(BF16)
        own = pl.ds(pl.multiple_of(me * slots, slots), slots)
        arrived[k, own, :] = placed[k, own, :]

    def a2a(k, c, i, to):
        peer = lax.rem(chip + i, n_chips) * 2 + to
        return pltpu.make_async_remote_copy(
            src_ref=placed.at[k, pl.ds(pl.multiple_of(peer * slots, slots), slots), cols(c)],
            dst_ref=arrived.at[k, pl.ds(pl.multiple_of(me * slots, slots), slots), cols(c)],
            send_sem=a2a_send.at[k, c, 2 * i + to],
            recv_sem=a2a_recv.at[k, c, 2 * i + core],
            device_id={"expert": peer},
            device_id_type=MESH,
        )

    def a2a_recv_wait(k, c, i, source):
        place = arrived.at[k, pl.ds(0, slots), cols(c)]
        pltpu.make_async_copy(place, place, a2a_recv.at[k, c, 2 * i + source]).wait()

    def a2a_start(k):
        for to in range(2):

            @pl.loop(0, chunks)
            def _(c):
                pl.when(core != to)(lambda: a2a(k, c, 0, to).start())

                @pl.loop(1, n_chips)
                def _(i):
                    a2a(k, c, i, to).start()

    def a2a_wait(k, c):
        a2a_recv_wait(k, c, 0, 1 - core)

        @pl.loop(1, n_chips)
        def _(i):
            for source in range(2):
                a2a_recv_wait(k, c, i, source)

    def a2a_end(k, c):
        a2a(k, c, 0, 1 - core).wait_send()

        @pl.loop(1, n_chips)
        def _(i):
            for to in range(2):
                a2a(k, c, i, to).wait_send()

    def crosses(q, side):
        beyond = lax.rem(spot + 1, ring) if side == 1 else lax.rem(ring - spot, ring)
        return beyond < HOPS[q]

    def hop(q, step, side, c):
        way = 2 * side - 1
        if step < HOPS[q] - 1:
            dst, target = relay.at[RELAY[q] + step, side, c], ring_at(way)
        else:
            dst, target = near.at[q, side, c], ring_at(way, jnp.where(crosses(q, side), 1, 0))
        return pltpu.make_async_remote_copy(
            src_ref=sent.at[q, c] if step == 0 else relay.at[RELAY[q] + step - 1, side, c],
            dst_ref=dst,
            send_sem=hop_send.at[BASE[q] + step, side, c],
            recv_sem=hop_recv.at[BASE[q] + step, side, c],
            device_id={"site": target},
            device_id_type=MESH,
        )

    def hop_start(q, c):
        for side in range(2):
            hop(q, 0, side, c).start()

    def first_start(c):
        for side in range(2):
            pl.when(spot != (0, ring - 1)[side])(lambda: hop(0, 0, side, c).start())

    def seam_start():
        for side in range(2):

            @pl.when(spot == (0, ring - 1)[side])
            def _():
                @pl.loop(0, chunks)
                def _(c):
                    hop(0, 0, side, c).start()

    def hop_wait(q, c):
        for side in range(2):
            hop(q, HOPS[q] - 1, side, c).wait_recv()

    def pass_on(q):
        for step in range(1, HOPS[q]):
            @pl.loop(0, chunks)
            def _(c):
                for side in range(2):
                    hop(q, step - 1, side, c).wait_recv()
                    hop(q, step, side, c).start()

    loads[0].wait()
    place(0)
    pl.semaphore_wait(barrier, n_experts + 1 + crossings)

    a2a_start(0)
    loads[1].wait()
    place(1)

    a2a_start(1)
    loads[2].wait()
    loads[3].wait()
    scale = 1.0 / math.sqrt(rows)

    @pl.loop(0, chunks)
    def _(c):
        off_load(c).wait()
        a2a_wait(0, c)
        g = (dot_tn(hid[0], arrived[0, :, cols(c)]) * scale).astype(BF16)
        grad[0, c] = g
        sent[0, c] = (off[c].astype(F32) + g.astype(F32)).astype(BF16)
        first_start(c)

    seam_start()

    def partner(q, c):
        flag = bits_ref[0, q]
        return jnp.where(flag == 1, near[q, 0, c].astype(F32), near[q, 1, c].astype(F32))

    fro[...] = jnp.zeros_like(fro)

    @pl.loop(0, chunks)
    def _(c):
        a2a_wait(1, c)
        late = (dot_tn(hid[1], arrived[1, :, cols(c)]) * scale).astype(BF16)
        grad[1, c] = late
        hop_wait(0, c)
        g = grad[0, c].astype(F32)
        summed = off[c].astype(F32) + g
        tracked = 0.5 * (summed + partner(0, c))
        second = (tracked - g).astype(BF16).astype(F32) + late.astype(F32)
        sent[1, c] = second.astype(BF16)
        hop_start(1, c)
        off[c] = (tracked - g).astype(BF16)
        tnorm[c] = tracked.astype(BF16)
        fro[...] += jnp.sum(tracked * tracked, axis=0, keepdims=True)

    def newton_schulz(finish):
        r = 1.0 / (jnp.sqrt(jnp.sum(fro[...], axis=1, keepdims=True)) + 1e-07)
        gram_b[...] = (gram[...] * (r * r)).astype(BF16)

        def polynomial():
            gb = gram_b[...]
            poly[...] = (coef_b * gb.astype(F32) + coef_c * dot_nn(gb, gb)).astype(BF16)

        polynomial()
        gram[...] = jnp.zeros_like(gram)

        @pl.loop(0, chunks)
        def _(c):
            t = tnorm[c]
            x = (r * (coef_a * t.astype(F32) + dot_nn(poly[...], t))).astype(BF16)
            xmid[c] = x
            gram[...] += dot_nt(x, x)

        gram_b[...] = gram[...].astype(BF16)
        polynomial()

        @pl.loop(0, chunks)
        def _(c):
            x = xmid[c]
            finish(c, (coef_a * x.astype(F32) + dot_nn(poly[...], x)).astype(BF16).astype(F32))

    gram[...] = jnp.zeros_like(gram)

    @pl.loop(0, chunks)
    def _(c):
        t = tnorm[c]
        gram[...] += dot_nt(t, t)

    for c in range(chunks):
        w_load(c).wait()

    def finish_first(c, ortho):
        moved[c] = wt[c].astype(F32) - step_scale * ortho

    newton_schulz(finish_first)

    pl.when(core == 1)(lambda: pl.semaphore_wait(turn, 1))
    pass_on(1)

    @pl.when(core == 0)
    def _():
        for side in range(2):
            hop(1, 1, side, chunks - 2).wait_send()
        pl.semaphore_signal(turn, inc=1, device_id={"expert": me + 1}, device_id_type=MESH)

    fro[...] = jnp.zeros_like(fro)
    gram[...] = jnp.zeros_like(gram)

    @pl.loop(0, chunks)
    def _(c):
        hop_wait(1, c)
        summed = off[c].astype(F32) + grad[1, c].astype(F32)
        tracked = 0.5 * (summed + partner(1, c))
        fro[...] += jnp.sum(tracked * tracked, axis=0, keepdims=True)
        t = tracked.astype(BF16)
        tnorm[c] = t
        gram[...] += dot_nt(t, t)

    def finish_second(c, ortho):
        m = moved[c] - step_scale * ortho
        sent[2, c] = m.astype(BF16)
        hop_start(2, c)
        moved[c] = m

    newton_schulz(finish_second)
    pass_on(2)

    @pl.loop(0, chunks)
    def _(c):
        hop_wait(2, c)
        beside = near[2, 0, c].astype(F32) + near[2, 1, c].astype(F32)
        out_ref[:, cols(c)] = (0.5 * moved[c] + 0.25 * beside).astype(BF16)

    @pl.loop(0, chunks)
    def _(c):
        for k in range(2):
            a2a_end(k, c)
        for q in range(3):
            for step in range(HOPS[q]):
                for side in range(2):
                    if (q, step) == (1, 1):
                        waited = (core == 0) & (c == chunks - 2)
                        pl.when(jnp.logical_not(waited))(lambda: hop(1, 1, side, c).wait_send())
                    else:
                        hop(q, step, side, c).wait_send()


def local(out_grads, routes, hiddens, weights, tracker_offset, partner_bits, chunk=CHUNK):
    n_experts = lax.axis_size("expert")
    n_sites = lax.axis_size("site")
    steps, _, tokens, features = out_grads.shape
    _, _, _, rows, ff = hiddens.shape
    chunks = features // chunk
    block = (chunks, ff, chunk)
    hbm = pl.BlockSpec(memory_space=pl.ANY)
    result = pl.pallas_call(
        functools.partial(kernel, n_sites, n_experts, chunk),
        out_shape=pltpu.VMEM((ff, features), BF16),
        in_specs=[
            hbm,
            pl.BlockSpec(memory_space=pltpu.VMEM),
            hbm,
            hbm,
            hbm,
            pl.BlockSpec(memory_space=pltpu.SMEM),
        ],
        out_specs=pl.BlockSpec(memory_space=pltpu.VMEM),
        scratch_shapes=[
            pltpu.VMEM((2, tokens, features), BF16),
            pltpu.VMEM((2, rows, ff), BF16),
            pltpu.VMEM(block, BF16),
            pltpu.VMEM(block, BF16),
            pltpu.VMEM((2, rows, features), BF16),
            pltpu.VMEM((2, rows, features), BF16),
            pltpu.VMEM((2,) + block, BF16),
            pltpu.VMEM((3,) + block, BF16),
            pltpu.VMEM((4, 2) + block, BF16),
            pltpu.VMEM((3, 2) + block, BF16),
            pltpu.VMEM(block, BF16),
            pltpu.VMEM(block, BF16),
            pltpu.VMEM(block, F32),
            pltpu.VMEM((ff, ff), F32),
            pltpu.VMEM((ff, ff), BF16),
            pltpu.VMEM((ff, ff), BF16),
            pltpu.VMEM((1, chunk), F32),
            pltpu.SemaphoreType.DMA((4 + 2 * chunks,)),
            pltpu.SemaphoreType.DMA((2, chunks, n_experts)),
            pltpu.SemaphoreType.DMA((2, chunks, n_experts)),
            pltpu.SemaphoreType.DMA((7, 2, chunks)),
            pltpu.SemaphoreType.DMA((7, 2, chunks)),
            pltpu.SemaphoreType.REGULAR,
        ],
        compiler_params=pltpu.CompilerParams(collective_id=0, has_side_effects=True, vmem_limit_bytes=61 << 20),
        name="gossip_muon",
    )(
        out_grads[:, 0],
        routes[:, 0, :, 0],
        hiddens[:, 0, 0],
        weights[0, 0],
        tracker_offset[0, 0],
        partner_bits,
    )
    return result[None, None]


def solution(mesh):
    in_specs = (
        P(None, "site", "expert", None),
        P(None, "site", "expert", None),
        P(None, "site", "expert", None, None),
        P("site", "expert", None, None),
        P("site", "expert", None, None),
        P("site", None),
    )
    out_specs = P("site", "expert", None, None)
    return jax.shard_map(local, mesh=mesh, in_specs=in_specs, out_specs=out_specs, check_vma=False)
```

profile of v0, /device:TPU:1, one launch (start us, length us, event | category | flops | bytes accessed | tf_op | source)
XLA Modules:
  0.0 188.8 jit_solution(8647791226349437565)
XLA Ops:
  0.0 187.8 %gossip_muon.1 = bf16[512,1024]{1,0:T(8,128)(2,1)S(1)} custom-call(bf16[2,128,1024]{2,1,0:T(8,128)(2,1)} %bitcast.9, s32[2,128]{1,0:T(2,128)} %bitcast.11, bf16[2,256,512]{2,1,0:T(8,128)(2,1)} %bitcast.10, bf16[512,1024]{1,0:T(8,128)(2,1)} %bitcast.7, bf16[512,1024]{1,0:T(8,128)(2,1)} %bitcast.8, s32[1,2]{1,0:T(1,128)} %bits_ref.1), custom_call_target="tpu_custom_call" | custom-call | tf_op jit(solution)/shard_map/gossip_muon/pallas_call | solution.py:352
  187.8 1.0 copy.8
where the time goes:
time: 189 us
  Pallas kernels  188 us (99%)
    pallas_call x1, Pallas kernels, local(): pl.pallas_call(functools.partial(kernel, n_sites, n_experts, chunk), out_...  188 us

commit v1 on v0

--- a/solution.py
+++ b/solution.py
@@ -30,14 +30,10 @@
     return lax.dot_general(a, b, (((1,), (1,)), ((), ())), preferred_element_type=F32)
 
 
-def dot_tn(a, b):
-    return lax.dot_general(a, b, (((0,), (0,)), ((), ())), preferred_element_type=F32)
-
-
 def kernel(
     n_sites, n_experts, chunk,
     og_hbm, routes_ref, hid_hbm, w_hbm, off_hbm, bits_ref, out_ref,
-    og, hid, wt, off, placed, arrived, grad, sent, relay, near, tnorm, xmid, moved,
+    og, hid, hid_t, wt, off, placed, arrived, grad, sent, relay, near, tnorm, xmid, moved,
     gram, gram_b, poly, fro,
     load_sem, a2a_send, a2a_recv, hop_send, hop_recv, turn,
 ):
@@ -208,24 +204,26 @@
     pl.semaphore_wait(barrier, n_experts + 1 + crossings)
 
     a2a_start(0)
+    loads[2].wait()
+    hid_t[0] = hid[0].T
     loads[1].wait()
     place(1)
 
     a2a_start(1)
-    loads[2].wait()
-    loads[3].wait()
     scale = 1.0 / math.sqrt(rows)
 
     @pl.loop(0, chunks)
     def _(c):
         off_load(c).wait()
         a2a_wait(0, c)
-        g = (dot_tn(hid[0], arrived[0, :, cols(c)]) * scale).astype(BF16)
+        g = (dot_nn(hid_t[0], arrived[0, :, cols(c)]) * scale).astype(BF16)
         grad[0, c] = g
         sent[0, c] = (off[c].astype(F32) + g.astype(F32)).astype(BF16)
         first_start(c)
 
     seam_start()
+    loads[3].wait()
+    hid_t[1] = hid[1].T
 
     def partner(q, c):
         flag = bits_ref[0, q]
@@ -236,7 +234,7 @@
     @pl.loop(0, chunks)
     def _(c):
         a2a_wait(1, c)
-        late = (dot_tn(hid[1], arrived[1, :, cols(c)]) * scale).astype(BF16)
+        late = (dot_nn(hid_t[1], arrived[1, :, cols(c)]) * scale).astype(BF16)
         grad[1, c] = late
         hop_wait(0, c)
         g = grad[0, c].astype(F32)
@@ -364,6 +362,7 @@
         scratch_shapes=[
             pltpu.VMEM((2, tokens, features), BF16),
             pltpu.VMEM((2, rows, ff), BF16),
+            pltpu.VMEM((2, ff, rows), BF16),
             pltpu.VMEM(block, BF16),
             pltpu.VMEM(block, BF16),
             pltpu.VMEM((2, rows, features), BF16),

time: 189 us -> 189 us (level)
  no operation moved by 1% of the time
where the time goes in v1:
time: 189 us
  Pallas kernels  188 us (99%)
    pallas_call x1, Pallas kernels, local(): pl.pallas_call(functools.partial(kernel, n_sites, n_experts, chunk), out_...  188 us

profile of v1, /device:TPU:1, one launch (start us, length us, event | category | flops | bytes accessed | tf_op | source)
XLA Modules:
  0.0 188.8 jit_solution(1764103120546140748)
XLA Ops:
  0.0 187.8 %gossip_muon.1 = bf16[512,1024]{1,0:T(8,128)(2,1)S(1)} custom-call(bf16[2,128,1024]{2,1,0:T(8,128)(2,1)} %bitcast.9, s32[2,128]{1,0:T(2,128)} %bitcast.11, bf16[2,256,512]{2,1,0:T(8,128)(2,1)} %bitcast.10, bf16[512,1024]{1,0:T(8,128)(2,1)} %bitcast.7, bf16[512,1024]{1,0:T(8,128)(2,1)} %bitcast.8, s32[1,2]{1,0:T(1,128)} %bits_ref.1), custom_call_target="tpu_custom_call" | custom-call | tf_op jit(solution)/shard_map/gossip_muon/pallas_call | solution.py:350
  187.8 1.0 copy.8
